TPU v7x, 256 devices: a whole 4x4x8 slice. The times are simulated.
256 devices in a mesh: ctx: 4 (over y), ch: 64 (over z, x, core).
Axes of the slice: x: 4, y: 4, z: 8, core: 2. Of those that a mesh axis runs over, the one named last changes fastest.
Arguments:
- query_gate: bfloat16 [4096, 8192], P('ch', 'ctx'), may hold values from -6 to 6
- key_gate: bfloat16 [4096, 8192], P('ch', 'ctx'), may hold values from -6 to 6
- value_proj: bfloat16 [4096, 8192], P('ch', 'ctx'), may hold values from -6 to 6
- filter_taps: bfloat16 [4096, 8192], P('ch'), may hold values from -0.0625 to 0.0625
- out_weight: bfloat16 [4096, 4096], P(None, 'ch'), may hold values from -0.09375 to 0.09375
Outputs:
- layer_out: bfloat16 [4096, 8192], P('ch', 'ctx')
All inputs are finite; a program needn't handle non-finite values.
Results may differ from a plain program's by a relative error of at most 0.015.
Values may be sent and summed in bfloat16 or wider, within the bound.
A program may use at most 128 MiB of HBM per device.

v0:
```python
import jax
import jax.numpy as jnp
import ml_dtypes
import numpy as np
from jax import lax
from jax.experimental import pallas as pl
from jax.experimental.pallas import tpu as pltpu
from jax.sharding import PartitionSpec as P

SEQ = 8192
N1 = 64
N2 = 128
CTX = 4
GROUP = 8
CHAN = 16
BATCH = 4

bf16 = jnp.bfloat16
f32 = jnp.float32


def two_parts(table):
    high = table.astype(ml_dtypes.bfloat16)
    low = (table - high.astype(np.float64)).astype(ml_dtypes.bfloat16)
    return high, low


def tables():
    root = np.pi / (2 * SEQ)
    n1, k1, n2, k2 = np.arange(N1), np.arange(N1), np.arange(N2), np.arange(N2)
    first = np.exp(1j * (root * N2 * n1[None, :] - 2 * np.pi * k1[:, None] * n1[None, :] / N1))
    twist = np.exp(1j * (root * n2[None, :] - 2 * np.pi * k1[:, None] * n2[None, :] / SEQ))
    second = np.exp(-2j * np.pi * n2[:, None] * k2[None, :] / N2)
    high, low = two_parts(np.concatenate([first.real, first.imag], axis=0))
    stage1 = np.concatenate([high, low], axis=1)
    fwd = two_parts(np.block([[second.real, second.imag], [-second.imag, second.real]]))
    inv = two_parts(np.block([[second.real, -second.imag], [second.imag, second.real]]))
    high, low = two_parts(np.concatenate([first.real.T, first.imag.T], axis=1) / SEQ)
    last = np.concatenate([high, low], axis=1)
    twist2 = np.concatenate([twist.real, twist.imag], axis=1).astype(np.float32)
    return stage1, np.stack(fwd), np.stack(inv), last, twist2


def dot(a, b):
    return jnp.dot(a, b, preferred_element_type=f32)


def parts_of(x):
    high = x.astype(bf16)
    return high, (x - high.astype(f32)).astype(bf16)


def dot3(x, table_ref):
    high, low = parts_of(x)
    return dot(high, table_ref[0]) + (dot(low, table_ref[0]) + dot(high, table_ref[1]))


def convolve(sig, filt, conv, stage1_ref, fwd_ref, inv_ref, last_ref, twist_ref):
    stage1 = stage1_ref[...]
    tw_re, tw_im = twist_ref[:, :N2], twist_ref[:, N2:]

    def spectrum(ref, c0):
        rows = []
        for c in range(BATCH):
            x = ref[pl.ds(c0 + c, N1, stride=CHAN), :].astype(bf16)
            a = dot(stage1, jnp.concatenate([x, x], axis=0))
            re, im = a[:N1], a[N1:]
            rows.append(
                jnp.concatenate([re * tw_re - im * tw_im, re * tw_im + im * tw_re], axis=1)
            )
        return dot3(jnp.concatenate(rows, axis=0), fwd_ref)

    def step(i, _):
        c0 = i * BATCH
        fs = spectrum(filt, c0)
        ss = spectrum(sig, c0)
        fr, fi, sr, si = fs[:, :N2], fs[:, N2:], ss[:, :N2], ss[:, N2:]
        prod = jnp.concatenate([fr * sr - fi * si, fr * si + fi * sr], axis=1)
        back = dot3(prod, inv_ref)
        last = last_ref[...]
        for c in range(BATCH):
            re = back[c * N1 : (c + 1) * N1, :N2]
            im = back[c * N1 : (c + 1) * N1, N2:]
            u = jnp.concatenate([re * tw_re + im * tw_im, im * tw_re - re * tw_im], axis=0)
            high, low = parts_of(u)
            y = dot(last, jnp.concatenate([high, high], axis=0)) + dot(last[:, :N2], low)
            conv[pl.ds(c0 + c, N1, stride=CHAN), :] = y
        return 0

    lax.fori_loop(0, CHAN // BATCH, step, 0)


def conv_kernel(p_ref, q_ref, f_ref, s1, fw, iv, la, tw, out_ref, sig, filt, conv):
    for n in range(N1):
        cols = slice(n * N2, (n + 1) * N2)
        sig[n * CHAN : (n + 1) * CHAN, :] = p_ref[:, cols].astype(f32)
        filt[n * CHAN : (n + 1) * CHAN, :] = f_ref[:, cols].astype(f32)
    convolve(sig, filt, conv, s1, fw, iv, la, tw)
    for n in range(N1):
        cols = slice(n * N2, (n + 1) * N2)
        out_ref[:, cols] = (
            q_ref[:, cols].astype(f32) * conv[n * CHAN : (n + 1) * CHAN, :]
        ).astype(bf16)


def gated_convolution(p, q, f):
    return pl.pallas_call(
        conv_kernel,
        out_shape=jax.ShapeDtypeStruct((CHAN, SEQ), bf16),
        scratch_shapes=[pltpu.VMEM((N1 * CHAN, N2), f32)] * 3,
        compiler_params=pltpu.CompilerParams(vmem_limit_bytes=32 * 1024 * 1024),
    )(p, q, f, *[jnp.asarray(t) for t in tables()])


def per_device(query_gate, key_gate, value_proj, filter_taps, out_weight):
    same_z = [[z * GROUP + j for j in range(GROUP)] for z in range(8)]
    same_j = [[z * GROUP + j for z in range(8)] for j in range(GROUP)]
    slab = lax.all_gather(out_weight.T, "ch", axis=0, tiled=True, axis_index_groups=same_z)
    product = (key_gate.astype(f32) * value_proj.astype(f32)).astype(bf16)
    both = jnp.stack([product, query_gate])
    both = lax.all_to_all(both, "ctx", split_axis=1, concat_axis=2, tiled=True)
    own = lax.axis_index("ctx") * CHAN
    taps = lax.dynamic_slice(filter_taps, (own, 0), (CHAN, SEQ))
    gated = gated_convolution(both[0], both[1], taps)
    gated = lax.all_to_all(gated, "ctx", split_axis=1, concat_axis=0, tiled=True)
    gated = lax.all_to_all(
        gated, "ch", split_axis=1, concat_axis=0, tiled=True, axis_index_groups=same_z
    )
    gated = lax.all_gather(gated, "ch", axis=0, tiled=True, axis_index_groups=same_j)
    out = jnp.dot(slab, gated, preferred_element_type=f32).astype(bf16)
    return lax.all_to_all(
        out, "ch", split_axis=0, concat_axis=1, tiled=True, axis_index_groups=same_z
    )


def solution(mesh):
    return jax.shard_map(
        per_device,
        mesh=mesh,
        in_specs=(P("ch", "ctx"), P("ch", "ctx"), P("ch", "ctx"), P("ch", None), P(None, "ch")),
        out_specs=P("ch", "ctx"),
        check_vma=False,
    )
```

profile of v0, /device:TPU:1, one launch (start us, length us, event | category | flops | bytes accessed | tf_op | source)
XLA Modules:
  0.0 148.2 jit_solution(10703421654418929247)
XLA Ops:
  6.6 0.0 copy-start.3
  6.6 1.2 fusion.1
  7.8 1.0 pad_maximum_fusion
  8.8 1.3 copy.27
  10.1 5.0 %all-to-all-start = ((bf16[2,64,2048]{2,0,1:T(2,128)(2,1)}), bf16[2,64,2048]{2,0,1:T(2,128)(2,1)S(1)}, u32[]{:S(2)}, u32[]{:S(2)}) async-start(bf16[2,64,2048]{2,0,1:T(2,128)(2,1)} %copy.27), calls=%async_computation | async-start | bytes 1048576 | tf_op jit(solution)/shard_map/all_to_all | solution.py:121
  15.1 0.0 copy-done
  15.2 7.5 %all-to-all-done = bf16[2,64,2048]{2,0,1:T(2,128)(2,1)S(1)} async-done(((bf16[2,64,2048]{2,0,1:T(2,128)(2,1)}), bf16[2,64,2048]{2,0,1:T(2,128)(2,1)S(1)}, u32[]{:S(2)}, u32[]{:S(2)}) %all-to-all-start) | async-done | bytes 524320 | tf_op jit(solution)/shard_map/all_to_all | solution.py:121
  22.7 0.4 copy.40
  23.1 0.2 fusion.2
  23.3 0.2 copy.35
  23.5 0.2 copy.36
  23.7 4.2 %shard_map.100 = bf16[16,8192]{1,0:T(8,128)(2,1)S(1)} custom-call(bf16[16,8192]{1,0:T(8,128)(2,1)S(1)} %bitcast.33, bf16[16,8192]{1,0:T(8,128)(2,1)S(1)} %bitcast.34, bf16[16,8192]{1,0:T(8,128)(2,1)S(1)} %constant_dynamic-slice_fusion.f_ref, bf16[128,128]{1,0:T(8,128)(2,1)S(1)} %copy-done.4, bf16[2,256,256]{2,1,0:T(8,128)(2,1)S(1)} %copy-done.1, ...), custom_call_target="tpu_custom_call" | custom-call | tf_op jit(solution)/shard_map/pallas_call | solution.py:107
  27.9 7.9 %all_to_all.69 = bf16[16,4,2048]{2,0,1:T(8,128)(2,1)S(1)} all-to-all(bf16[16,4,2048]{2,0,1:T(8,128)(2,1)S(1)} %bitcast.39), channel_id=1, replica_groups=mesh['ctx'=4,'ch'=64] {'ctx'}, dimensions={1} | all-to-all | bytes 524288 | tf_op jit(solution)/shard_map/all_to_all | solution.py:125
  35.8 0.1 copy.37
  35.9 14.7 %all_to_all.70 = bf16[64,8,256]{2,0,1:T(8,128)(2,1)} all-to-all(bf16[64,8,256]{2,0,1:T(8,128)(2,1)S(1)} %copy.30), channel_id=1, replica_groups={{0,1,2,3,4,5,6,7},{8,9,10,11,12,13,14,15},{16,17,18,19,20,21,22,23},{24..., dimensions={1} | all-to-all | bytes 524288 | tf_op jit(solution)/shard_map/all_to_all | solution.py:126
  50.7 0.0 all-gather.3.cloned.1.call-update
  50.7 0.0 all-gather.5.cloned.1.call-start
  50.8 0.7 all-gather.5.cloned.1.call-update
  51.5 36.3 %all-gather.3.cloned.1.call-done = bf16[4096,256]{1,0:T(8,128)(2,1)} async-done(((bf16[512,256]{1,0:T(8,128)(2,1)}), bf16[4096,256]{1,0:T(8,128)(2,1)}) %all-gather.3.cloned.1.call-update) | async-done | bytes 2097168 | tf_op jit(solution)/shard_map/all_gather | solution.py:129
  87.7 39.2 %all-gather.5.cloned.1.call-done = bf16[512,4096]{1,0:T(8,128)(2,1)} async-done(((bf16[64,4096]{1,0:T(8,128)(2,1)}), bf16[512,4096]{1,0:T(8,128)(2,1)}) %all-gather.5.cloned.1.call-update) | async-done | bytes 4194320 | tf_op jit(solution)/shard_map/all_gather | solution.py:118
  126.9 4.1 %fusion = bf16[512,256]{0,1:T(8,128)(2,1)S(1)} fusion(bf16[4096,256]{1,0:T(8,128)(2,1)} %all-gather.3.cloned.1.call-done, bf16[512,4096]{1,0:T(8,128)(2,1)} %all-gather.5.cloned.1.call-done), kind=kOutput, calls=%fused_computation.1 | convolution fusion | flops 1073872896 | bytes 6553600 | tf_op jit(solution)/shard_map/dot_general | solution.py:130
  131.0 0.1 copy.31
  131.2 9.5 %all_to_all.71 = bf16[8,64,256]{2,1,0:T(8,128)(2,1)S(1)} all-to-all(bf16[8,64,256]{2,1,0:T(8,128)(2,1)S(1)} %bitcast.42), channel_id=1, replica_groups={{0,1,2,3,4,5,6,7},{8,9,10,11,12,13,14,15},{16,17,18,19,20,21,22,23},{24..., dimensions={0} | all-to-all | bytes 524288 | tf_op jit(solution)/shard_map/all_to_all | solution.py:131
  140.7 0.7 copy.34
  (14 shorter events, 0.1 us)
Async XLA Ops:
  6.5 8.6 %copy-start = (bf16[64,8192]{1,0:T(8,128)(2,1)S(1)}, bf16[64,8192]{1,0:T(8,128)(2,1)}, u32[]{:S(2)}) copy-start(bf16[64,8192]{1,0:T(8,128)(2,1)} %param.13) | copy-start | bytes 3145732
  6.5 17.1 %copy-start.4 = (bf16[128,128]{1,0:T(8,128)(2,1)S(1)}, bf16[128,128]{1,0:T(8,128)(2,1)}, u32[]{:S(2)}) copy-start(bf16[128,128]{1,0:T(8,128)(2,1)} %constant.22.clone.s1) | copy-start | bytes 98308
  6.5 17.1 %copy-start.1 = (bf16[2,256,256]{2,1,0:T(8,128)(2,1)S(1)}, bf16[2,256,256]{2,1,0:T(8,128)(2,1)}, u32[]{:S(2)}) copy-start(bf16[2,256,256]{2,1,0:T(8,128)(2,1)} %constant.23.clone.fw) | copy-start | bytes 786436
  6.5 17.1 %copy-start.2 = (bf16[2,256,256]{2,1,0:T(8,128)(2,1)S(1)}, bf16[2,256,256]{2,1,0:T(8,128)(2,1)}, u32[]{:S(2)}) copy-start(bf16[2,256,256]{2,1,0:T(8,128)(2,1)} %constant.24.clone.iv) | copy-start | bytes 786436
  6.5 17.1 %copy-start.5 = (bf16[64,256]{1,0:T(8,128)(2,1)S(1)}, bf16[64,256]{1,0:T(8,128)(2,1)}, u32[]{:S(2)}) copy-start(bf16[64,256]{1,0:T(8,128)(2,1)} %constant.25.clone.la) | copy-start | bytes 98308
  6.6 17.1 %copy-start.3 = (f32[64,256]{1,0:T(8,128)S(1)}, f32[64,256]{1,0:T(8,128)}, u32[]{:S(2)}) copy-start(f32[64,256]{1,0:T(8,128)} %constant.26.clone.tw) | copy-start | bytes 196612
  10.1 12.6 %all-to-all-start = ((bf16[2,64,2048]{2,0,1:T(2,128)(2,1)}), bf16[2,64,2048]{2,0,1:T(2,128)(2,1)S(1)}, u32[]{:S(2)}, u32[]{:S(2)}) async-start(bf16[2,64,2048]{2,0,1:T(2,128)(2,1)} %copy.27), calls=%async_computation | async-start | bytes 1048576 | tf_op jit(solution)/shard_map/all_to_all | solution.py:121
  15.1 72.6 %all-gather.3.cloned.1.call-start = ((), (), s32[]{:S(2)}) async-start(), calls=%async_computation.4 | async-start | bytes 2359296 | tf_op jit(solution)/shard_map/all_gather | solution.py:129
  50.7 76.2 %all-gather.5.cloned.1.call-start = ((), (), s32[]{:S(2)}) async-start(), calls=%async_computation.5 | async-start | bytes 4718592 | tf_op jit(solution)/shard_map/all_gather | solution.py:118
Sparse Core Ops, SparseCore 0:
  50.8 36.8 all-gather.2
  89.6 37.2 all-gather.4
where the time goes:
time: 149 us; the launch traced here: 148 us
  waiting for transfers between devices  83.7 us (56%)
  blocking collectives  32.2 us (22%)
  between operations  13.5 us (9%)
  starting transfers between devices  5.06 us (3%)
  Pallas kernels  4.2 us (3%)
  matrix products  4.12 us (3%)
  local copies, waits for them, and re-layouts  3.27 us (2%)
  other arithmetic  2.21 us (1%)
    all_gather x1, waiting for transfers between devices, per_device(): lax.all_gather(out_weight.T, 'ch', axis=0, tiled=True, axis_index_groups=...  39.2 us
    all_gather x1, waiting for transfers between devices, per_device(): lax.all_gather(gated, 'ch', axis=0, tiled=True, axis_index_groups=same_j)  36.3 us
    all_to_all x1, blocking collectives, per_device(): lax.all_to_all(gated, 'ch', split_axis=1, concat_axis=0, tiled=True, axis...  14.7 us
    all_to_all x1, blocking collectives, per_device(): lax.all_to_all(out, 'ch', split_axis=0, concat_axis=1, tiled=True, axis_i...  9.51 us
    all_to_all x1, blocking collectives, per_device(): lax.all_to_all(gated, 'ctx', split_axis=1, concat_axis=0, tiled=True)  7.92 us
    all_to_all x1, waiting for transfers between devices, per_device(): both = lax.all_to_all(both, 'ctx', split_axis=1, concat_axis=2, tiled=True)  7.52 us
    all_to_all x1, starting transfers between devices, per_device(): both = lax.all_to_all(both, 'ctx', split_axis=1, concat_axis=2, tiled=True)  5.01 us
    pallas_call x1, Pallas kernels, gated_convolution(): pl.pallas_call(conv_kernel, out_shape=jax.ShapeDtypeStruct((CHAN, SEQ), b...  4.2 us
  transfers between devices with their start and end apart: 3, of which 3 were waited for; matrix products, arithmetic and copies ran while one was open for 0% of the time, Pallas kernels for 0%

commit v1 on v0

v1 whole, which is shorter than its diff:
```python
import jax
import jax.numpy as jnp
import ml_dtypes
import numpy as np
from jax import lax
from jax.experimental import pallas as pl
from jax.experimental.pallas import tpu as pltpu
from jax.sharding import PartitionSpec as P

SEQ = 8192
N1 = 64
N2 = 128
CTX = 4
GROUP = 8
CHAN = 16
BATCH = 4
RING = 8
PLANE = CTX * GROUP
TOK = 256
D = 4096
SLAB = D // RING
MESH = pl.DeviceIdType.MESH

bf16 = jnp.bfloat16
f32 = jnp.float32


def two_parts(table):
    high = table.astype(ml_dtypes.bfloat16)
    low = (table - high.astype(np.float64)).astype(ml_dtypes.bfloat16)
    return high, low


def tables():
    root = np.pi / (2 * SEQ)
    n1, k1, n2, k2 = np.arange(N1), np.arange(N1), np.arange(N2), np.arange(N2)
    first = np.exp(1j * (root * N2 * n1[None, :] - 2 * np.pi * k1[:, None] * n1[None, :] / N1))
    twist = np.exp(1j * (root * n2[None, :] - 2 * np.pi * k1[:, None] * n2[None, :] / SEQ))
    second = np.exp(-2j * np.pi * n2[:, None] * k2[None, :] / N2)
    high, low = two_parts(np.concatenate([first.real, first.imag], axis=0))
    stage1 = np.concatenate([high, low], axis=1)
    fwd = two_parts(np.block([[second.real, second.imag], [-second.imag, second.real]]))
    inv = two_parts(np.block([[second.real, -second.imag], [second.imag, second.real]]))
    high, low = two_parts(np.concatenate([first.real.T, first.imag.T], axis=1) / SEQ)
    last = np.concatenate([high, low], axis=1)
    twist2 = np.concatenate([twist.real, twist.imag], axis=1).astype(np.float32)
    return stage1, np.stack(fwd), np.stack(inv), last, twist2


def dot(a, b):
    return jnp.dot(a, b, preferred_element_type=f32)


def parts_of(x):
    high = x.astype(bf16)
    return high, (x - high.astype(f32)).astype(bf16)


def dot3(x, table_ref):
    high, low = parts_of(x)
    return dot(high, table_ref[0]) + (dot(low, table_ref[0]) + dot(high, table_ref[1]))


def spectrum(ref, c0, stage1, tw_re, tw_im, fwd_ref):
    rows = []
    for c in range(BATCH):
        x = ref[pl.ds(c0 + c, N1, stride=CHAN), :].astype(bf16)
        a = dot(stage1, jnp.concatenate([x, x], axis=0))
        re, im = a[:N1], a[N1:]
        rows.append(jnp.concatenate([re * tw_re - im * tw_im, re * tw_im + im * tw_re], axis=1))
    return dot3(jnp.concatenate(rows, axis=0), fwd_ref)


def layer_kernel(
    q_ref, k_ref, v_ref, f_ref, w_ref, s1_ref, fwd_ref, inv_ref, last_ref, tw_ref,
    out_ref,
    prod, pbuf, qbuf, sig, filt, conv, fspec, gsend, gbuf, wbuf, acc, osend, obuf,
    p_send, p_recv, q_send, q_recv, w_send, w_recv, s_send, s_recv,
    g_send, g_recv, r_send, r_recv, l_send, l_recv, o_send, o_recv,
):
    ctx = lax.axis_index("ctx")
    ch = lax.axis_index("ch")
    z, j = ch // GROUP, ch % GROUP
    x, core = j // 2, j % 2
    me = ctx * GROUP + j

    def at(other_ctx, other_z, other_j):
        return (other_ctx, other_z * GROUP + other_j)

    def send(src, dst, send_sem, recv_sem, device):
        copy = pltpu.make_async_remote_copy(
            src_ref=src, dst_ref=dst, send_sem=send_sem, recv_sem=recv_sem,
            device_id=device, device_id_type=MESH,
        )
        copy.start()
        return copy

    up, down = at(ctx, (z + 1) % RING, j), at(ctx, (z + RING - 1) % RING, j)
    barrier = pltpu.get_barrier_semaphore()

    def greet(i, _):
        peer = (me + 1 + i) % PLANE
        pl.semaphore_signal(
            barrier, inc=1, device_id=at(peer // GROUP, z, peer % GROUP), device_id_type=MESH
        )
        return 0

    lax.fori_loop(0, PLANE - 1, greet, 0)
    pl.semaphore_signal(barrier, inc=1, device_id=up, device_id_type=MESH)
    pl.semaphore_signal(barrier, inc=1, device_id=down, device_id_type=MESH)

    prod[...] = (k_ref[...].astype(f32) * v_ref[...].astype(f32)).astype(bf16)
    pl.semaphore_wait(barrier, PLANE + 1)

    waits = []
    for refs in ((prod, pbuf, p_send, p_recv), (q_ref, qbuf, q_send, q_recv)):
        src, dst, send_sem, recv_sem = refs
        for i in range(1, CTX):
            peer = (ctx + i) % CTX
            waits.append(
                send(src.at[peer], dst.at[ctx], send_sem.at[i], recv_sem.at[i], at(peer, z, j))
            )
    p_waits, q_waits = waits[: CTX - 1], waits[CTX - 1 :]
    pbuf[ctx] = prod[ctx]
    qbuf[ctx] = q_ref[ctx]

    def turn(i, _):
        rows = pl.ds(pl.multiple_of(i * 128, 128), 128)
        wbuf[j, :, rows] = w_ref[rows, :].astype(f32).T.astype(bf16)
        return 0

    lax.fori_loop(0, D // 128, turn, 0)
    xr, xl = (x + 1) % 4, (x + 3) % 4
    right, left = at(ctx, z, xr * 2 + core), at(ctx, z, xl * 2 + core)
    sibling = at(ctx, z, x * 2 + 1 - core)
    j_right, j_left, j_far = xr * 2 + core, xl * 2 + core, ((x + 2) % 4) * 2 + core
    w_waits = [
        send(wbuf.at[j], wbuf.at[j], w_send.at[0], w_recv.at[0], right),
        send(wbuf.at[j], wbuf.at[j], w_send.at[1], w_recv.at[1], left),
    ]
    s_waits = [send(wbuf.at[j], wbuf.at[j], s_send.at[0], s_recv.at[0], sibling)]

    own = pl.ds(pl.multiple_of(ctx * CHAN, CHAN), CHAN)
    for n in range(N1):
        filt[n * CHAN : (n + 1) * CHAN, :] = f_ref[own, n * N2 : (n + 1) * N2].astype(f32)
    stage1 = s1_ref[...]
    tw_re, tw_im = tw_ref[:, :N2], tw_ref[:, N2:]

    def filter_step(i, _):
        fspec[i] = spectrum(filt, i * BATCH, stage1, tw_re, tw_im, fwd_ref)
        return 0

    lax.fori_loop(0, CHAN // BATCH, filter_step, 0)

    for copy in p_waits:
        copy.wait_recv()
    for n in range(N1):
        col = (n % 16) * N2
        sig[n * CHAN : (n + 1) * CHAN, :] = pbuf[n // 16, :, col : col + N2].astype(f32)

    def conv_step(i, _):
        c0 = i * BATCH
        fs = fspec[i]
        ss = spectrum(sig, c0, stage1, tw_re, tw_im, fwd_ref)
        fr, fi, sr, si = fs[:, :N2], fs[:, N2:], ss[:, :N2], ss[:, N2:]
        back = dot3(jnp.concatenate([fr * sr - fi * si, fr * si + fi * sr], axis=1), inv_ref)
        last = last_ref[...]
        for c in range(BATCH):
            re = back[c * N1 : (c + 1) * N1, :N2]
            im = back[c * N1 : (c + 1) * N1, N2:]
            u = jnp.concatenate([re * tw_re + im * tw_im, im * tw_re - re * tw_im], axis=0)
            high, low = parts_of(u)
            y = dot(last, jnp.concatenate([high, high], axis=0)) + dot(last[:, :N2], low)
            conv[pl.ds(c0 + c, N1, stride=CHAN), :] = y
        return 0

    lax.fori_loop(0, CHAN // BATCH, conv_step, 0)

    for copy in q_waits:
        copy.wait_recv()
    for n in range(N1):
        col = (n % 16) * N2
        gate = qbuf[n // 16, :, col : col + N2].astype(f32)
        gsend[n // 2, :, (n % 2) * N2 : (n % 2 + 1) * N2] = (
            gate * conv[n * CHAN : (n + 1) * CHAN, :]
        ).astype(bf16)

    slot = j * CTX + ctx

    def tile_copy(i):
        peer = (me + i) % PLANE
        return pltpu.make_async_remote_copy(
            src_ref=gsend.at[peer], dst_ref=gbuf.at[z, slot], send_sem=g_send.at[i],
            recv_sem=g_recv.at[slot], device_id=at(peer // GROUP, z, peer % GROUP),
            device_id_type=MESH,
        )

    def scatter(i, _):
        tile_copy(i).start()
        return 0

    lax.fori_loop(1, PLANE, scatter, 0)
    gbuf[z, slot] = gsend[me]

    def arrived(i, _):
        @pl.when(i != slot)
        def _():
            pltpu.make_async_remote_copy(
                src_ref=gsend.at[0], dst_ref=gbuf.at[z, i], send_sem=g_send.at[0],
                recv_sem=g_recv.at[i], device_id=up, device_id_type=MESH,
            ).wait_recv()

        return 0

    half = PLANE // 2

    def pass_on(step, h):
        rows = pl.ds(h * half, half)
        up_slab, down_slab = (z + RING - step) % RING, (z + step) % RING
        ups = downs = None
        if step < 3 or h == 0:
            part = gbuf.at[up_slab, rows]
            ups = send(part, part, r_send.at[step, h], r_recv.at[step, h], up)
        if step < 3 or h == 1:
            part = gbuf.at[down_slab, rows]
            downs = send(part, part, l_send.at[step, h], l_recv.at[step, h], down)
        return ups, downs

    hops = {}
    for h in range(2):
        lax.fori_loop(h * half, (h + 1) * half, arrived, 0)
        hops[0, h] = pass_on(0, h)

    w_waits[0].wait_recv()
    part = wbuf.at[j_left, pl.ds(0, 32)]
    w_waits.append(send(part, part, w_send.at[2], w_recv.at[2], right))
    part = wbuf.at[j_left]
    s_waits.append(send(part, part, s_send.at[1], s_recv.at[1], sibling))
    w_waits[1].wait_recv()
    part = wbuf.at[j_right, pl.ds(32, 32)]
    w_waits.append(send(part, part, w_send.at[3], w_recv.at[3], left))
    part = wbuf.at[j_right]
    s_waits.append(send(part, part, s_send.at[2], s_recv.at[2], sibling))

    def take(step):
        for h in range(2):
            ups, downs = hops[step, h]
            if ups is not None:
                ups.wait_recv()
            if downs is not None:
                downs.wait_recv()
            if step < 3:
                hops[step + 1, h] = pass_on(step + 1, h)

    def project(offset, first=False):
        slab = (z + offset) % RING
        cols = pl.ds(pl.multiple_of(slab * SLAB, SLAB), SLAB)
        weight = wbuf[:, :, cols].reshape(SLAB, SLAB)
        term = dot(weight, gbuf[slab].reshape(SLAB, TOK))
        acc[...] = term if first else acc[...] + term

    take(0)
    w_waits[2].wait_recv()
    w_waits[3].wait_recv()
    part = wbuf.at[j_far]
    s_waits.append(send(part, part, s_send.at[3], s_recv.at[3], sibling))
    take(1)
    for copy in s_waits:
        copy.wait_recv()
    project(0, first=True)
    project(1)
    project(RING - 1)
    take(2)
    project(2)
    project(RING - 2)
    project(3)
    project(RING - 3)
    take(3)
    project(4)

    osend[...] = acc[...].reshape(GROUP, 64, TOK).astype(bf16)
    o_waits = []
    for i in range(1, GROUP):
        peer = (j + i) % GROUP
        o_waits.append(
            send(osend.at[peer], obuf.at[j], o_send.at[i], o_recv.at[i], at(ctx, z, peer))
        )
    obuf[j] = osend[j]
    for copy in o_waits:
        copy.wait_recv()
    for i in range(GROUP):
        out_ref[:, i * TOK : (i + 1) * TOK] = obuf[i]

    for copy in p_waits + q_waits + w_waits + s_waits + o_waits:
        copy.wait_send()
    for ups, downs in hops.values():
        if ups is not None:
            ups.wait_send()
        if downs is not None:
            downs.wait_send()

    def sent(i, _):
        tile_copy(i).wait_send()
        return 0

    lax.fori_loop(1, PLANE, sent, 0)


def per_device(query_gate, key_gate, value_proj, filter_taps, out_weight):
    tokens = SEQ // CTX
    split = (CTX, CHAN, tokens)
    dma = pltpu.SemaphoreType.DMA
    return pl.pallas_call(
        layer_kernel,
        out_shape=jax.ShapeDtypeStruct((CTX * CHAN, tokens), bf16),
        in_specs=[pl.BlockSpec(memory_space=pltpu.VMEM)] * 10,
        out_specs=pl.BlockSpec(memory_space=pltpu.VMEM),
        scratch_shapes=[
            pltpu.VMEM(split, bf16),
            pltpu.VMEM(split, bf16),
            pltpu.VMEM(split, bf16),
            pltpu.VMEM((N1 * CHAN, N2), f32),
            pltpu.VMEM((N1 * CHAN, N2), f32),
            pltpu.VMEM((N1 * CHAN, N2), f32),
            pltpu.VMEM((CHAN // BATCH, BATCH * N1, 2 * N2), f32),
            pltpu.VMEM((PLANE, CHAN, TOK), bf16),
            pltpu.VMEM((RING, PLANE, CHAN, TOK), bf16),
            pltpu.VMEM((GROUP, 64, D), bf16),
            pltpu.VMEM((SLAB, TOK), f32),
            pltpu.VMEM((GROUP, 64, TOK), bf16),
            pltpu.VMEM((GROUP, 64, TOK), bf16),
            dma((CTX,)), dma((CTX,)), dma((CTX,)), dma((CTX,)),
            dma((4,)), dma((4,)), dma((4,)), dma((4,)),
            dma((PLANE,)), dma((PLANE,)),
            dma((4, 2)), dma((4, 2)), dma((4, 2)), dma((4, 2)),
            dma((GROUP,)), dma((GROUP,)),
        ],
        compiler_params=pltpu.CompilerParams(
            collective_id=0, has_side_effects=True, vmem_limit_bytes=48 * 1024 * 1024
        ),
    )(
        query_gate.reshape(split),
        key_gate.reshape(split),
        value_proj.reshape(split),
        filter_taps,
        out_weight,
        *[jnp.asarray(t) for t in tables()],
    )


def solution(mesh):
    return jax.shard_map(
        per_device,
        mesh=mesh,
        in_specs=(P("ch", "ctx"), P("ch", "ctx"), P("ch", "ctx"), P("ch", None), P(None, "ch")),
        out_specs=P("ch", "ctx"),
        check_vma=False,
    )
```

time: 149 us -> 67.9 us (0.46)
  waiting for transfers between devices: 83.7 us -> 0 us
  Pallas kernels: 4.2 us -> 60 us
  blocking collectives: 32.2 us -> 0 us
  between operations: 13.5 us -> 0.06 us
  starting transfers between devices: 5.06 us -> 0 us
  local copies, waits for them, and re-layouts: 3.27 us -> 7.55 us
  matrix products: 4.12 us -> 0 us
  other arithmetic: 2.21 us -> 0 us
    all_gather x2 -> x0, waiting for transfers between devices: 75.5 us -> none  [the longest x1 39.2 us: per_device(): lax.all_gather(out_weight.T, 'ch', axis=0, tiled=True, axis_index_groups=...]
    pallas_call x1, Pallas kernels: 4.2 us -> 60 us  [per_device(): pl.pallas_call(layer_kernel, out_shape=jax.ShapeDtypeStruct((CTX * CHAN,...]
    all_to_all x3 -> x0, blocking collectives: 32.2 us -> none  [the longest x1 14.7 us: per_device(): lax.all_to_all(gated, 'ch', split_axis=1, concat_axis=0, tiled=True, axis...]
    all_to_all x1 -> x0, waiting for transfers between devices: 7.52 us -> none  [per_device(): both = lax.all_to_all(both, 'ctx', split_axis=1, concat_axis=2, tiled=True)]
    unnamed x15 -> x20, local copies, waits for them, and re-layouts: 0.38 us -> 7.55 us
    all_to_all x1 -> x0, starting transfers between devices: 5.01 us -> none  [per_device(): both = lax.all_to_all(both, 'ctx', split_axis=1, concat_axis=2, tiled=True)]
    dot_general x1 -> x0, matrix products: 4.12 us -> none  [per_device(): out = jnp.dot(slab, gated, preferred_element_type=f32).astype(bf16)]
    another operation x2 -> x0, other arithmetic: 2.21 us -> none  [per_device(): both = jnp.stack([product, query_gate])]
  transfers between devices with their start and end apart: 3 -> 0, of which waited for: 3 -> 0; matrix products, arithmetic and copies ran while one was open for 0% -> 0% of each run, Pallas kernels for 0% -> 0%
where the time goes in v1:
time: 67.9 us; the launch traced here: 67.6 us
  Pallas kernels  60 us (88%)
  local copies, waits for them, and re-layouts  7.55 us (11%)
    pallas_call x1, Pallas kernels, per_device(): pl.pallas_call(layer_kernel, out_shape=jax.ShapeDtypeStruct((CTX * CHAN,...  60 us
    unnamed x20, local copies, waits for them, and re-layouts  7.55 us

profile of v1, /device:TPU:1, one launch (start us, length us, event | category | flops | bytes accessed | tf_op | source)
XLA Modules:
  0.0 67.6 jit_solution(2051965649300187516)
XLA Ops:
  0.0 0.0 copy-start
  0.0 0.0 copy-start.1
  0.0 0.0 copy-start.2
  0.0 1.6 %copy.11.w_ref = bf16[4096,64]{1,0:T(8,128)(2,1)S(1)} copy(bf16[4096,64]{0,1:T(8,128)(2,1)} %param.14) | data formatting | bytes 1048576 | tf_op args[4]
  1.6 0.0 copy-done
  1.7 0.0 copy-done.1
  1.7 0.0 copy-done.2
  1.7 0.0 copy-start.3
  1.7 0.9 %copy-done.3 = bf16[64,2048]{1,0:T(8,128)(2,1)S(1)} copy-done((bf16[64,2048]{1,0:T(8,128)(2,1)S(1)}, bf16[64,2048]{1,0:T(8,128)(2,1)}, u32[]{:S(2)}) %copy-start.3) | copy-done | bytes 262168
  2.6 0.0 copy-start.4
  2.6 0.9 %copy-done.4 = bf16[2,256,256]{2,1,0:T(8,128)(2,1)S(1)} copy-done((bf16[2,256,256]{2,1,0:T(8,128)(2,1)S(1)}, bf16[2,256,256]{2,1,0:T(8,128)(2,1)}, u32[]{:S(2)}) %copy-start.4) | copy-done | bytes 262168
  3.6 0.0 copy-start.5
  3.6 0.9 %copy-done.5 = bf16[2,256,256]{2,1,0:T(8,128)(2,1)S(1)} copy-done((bf16[2,256,256]{2,1,0:T(8,128)(2,1)S(1)}, bf16[2,256,256]{2,1,0:T(8,128)(2,1)}, u32[]{:S(2)}) %copy-start.5) | copy-done | bytes 262168
  4.5 0.0 copy-start.6
  4.5 0.8 %copy-done.6 = f32[64,256]{1,0:T(8,128)S(1)} copy-done((f32[64,256]{1,0:T(8,128)S(1)}, f32[64,256]{1,0:T(8,128)}, u32[]{:S(2)}) %copy-start.6) | copy-done | bytes 65560
  5.4 0.0 copy-start.7
  5.4 0.8 %copy-done.7 = bf16[64,256]{1,0:T(8,128)(2,1)S(1)} copy-done((bf16[64,256]{1,0:T(8,128)(2,1)S(1)}, bf16[64,256]{1,0:T(8,128)(2,1)}, u32[]{:S(2)}) %copy-start.7) | copy-done | bytes 32792
  6.1 0.0 copy-start.8
  6.1 0.8 %copy-done.8 = bf16[128,128]{1,0:T(8,128)(2,1)S(1)} copy-done((bf16[128,128]{1,0:T(8,128)(2,1)S(1)}, bf16[128,128]{1,0:T(8,128)(2,1)}, u32[]{:S(2)}) %copy-start.8) | copy-done | bytes 32792
  6.9 60.0 %shard_map.100 = bf16[64,2048]{1,0:T(8,128)(2,1)S(1)} custom-call(bf16[4,16,2048]{2,1,0:T(8,128)(2,1)S(1)} %bitcast.3, bf16[4,16,2048]{2,1,0:T(8,128)(2,1)S(1)} %bitcast.4, bf16[4,16,2048]{2,1,0:T(8,128)(2,1)S(1)} %bitcast.5, bf16[64,8192]{1,0:T(8,128)(2,1)S(1)} %copy-done, bf16[4096,64]{1,0:T(8,128)(2,1)S(1)} %copy.11.w_ref, ...), custom_call_target="tpu_custom_call" | custom-call | tf_op jit(solution)/shard_map/pallas_call | solution.py:313
  66.9 0.7 %copy.13 = bf16[64,2048]{1,0:T(8,128)(2,1)} copy(bf16[64,2048]{1,0:T(8,128)(2,1)S(1)} %shard_map.100) | data formatting | bytes 524288
Async XLA Ops:
  0.0 1.7 %copy-start = (bf16[64,8192]{1,0:T(8,128)(2,1)S(1)}, bf16[64,8192]{1,0:T(8,128)(2,1)}, u32[]{:S(2)}) copy-start(bf16[64,8192]{1,0:T(8,128)(2,1)} %f_ref.1) | copy-start | bytes 3145732
  0.0 1.7 %copy-start.1 = (bf16[64,2048]{1,0:T(8,128)(2,1)S(1)}, bf16[64,2048]{1,0:T(8,128)(2,1)}, u32[]{:S(2)}) copy-start(bf16[64,2048]{1,0:T(8,128)(2,1)} %param.10) | copy-start | bytes 786436
  0.0 1.7 %copy-start.2 = (bf16[64,2048]{1,0:T(8,128)(2,1)S(1)}, bf16[64,2048]{1,0:T(8,128)(2,1)}, u32[]{:S(2)}) copy-start(bf16[64,2048]{1,0:T(8,128)(2,1)} %param.11) | copy-start | bytes 786436
  1.7 1.0 %copy-start.3 = (bf16[64,2048]{1,0:T(8,128)(2,1)S(1)}, bf16[64,2048]{1,0:T(8,128)(2,1)}, u32[]{:S(2)}) copy-start(bf16[64,2048]{1,0:T(8,128)(2,1)} %param.12) | copy-start | bytes 786436
  2.6 0.9 %copy-start.4 = (bf16[2,256,256]{2,1,0:T(8,128)(2,1)S(1)}, bf16[2,256,256]{2,1,0:T(8,128)(2,1)}, u32[]{:S(2)}) copy-start(bf16[2,256,256]{2,1,0:T(8,128)(2,1)} %constant.12.clone.inv_ref) | copy-start | bytes 786436
  3.6 0.9 %copy-start.5 = (bf16[2,256,256]{2,1,0:T(8,128)(2,1)S(1)}, bf16[2,256,256]{2,1,0:T(8,128)(2,1)}, u32[]{:S(2)}) copy-start(bf16[2,256,256]{2,1,0:T(8,128)(2,1)} %constant.11.clone.fwd_ref) | copy-start | bytes 786436
  4.5 0.8 %copy-start.6 = (f32[64,256]{1,0:T(8,128)S(1)}, f32[64,256]{1,0:T(8,128)}, u32[]{:S(2)}) copy-start(f32[64,256]{1,0:T(8,128)} %constant.14.clone.tw_ref) | copy-start | bytes 196612
  5.4 0.8 %copy-start.7 = (bf16[64,256]{1,0:T(8,128)(2,1)S(1)}, bf16[64,256]{1,0:T(8,128)(2,1)}, u32[]{:S(2)}) copy-start(bf16[64,256]{1,0:T(8,128)(2,1)} %constant.13.clone.last_ref) | copy-start | bytes 98308
  6.1 0.8 %copy-start.8 = (bf16[128,128]{1,0:T(8,128)(2,1)S(1)}, bf16[128,128]{1,0:T(8,128)(2,1)}, u32[]{:S(2)}) copy-start(bf16[128,128]{1,0:T(8,128)(2,1)} %constant.10.clone.s1_ref) | copy-start | bytes 98308

commit v2 on v1

--- a/solution.py
+++ b/solution.py
@@ -72,9 +72,11 @@
 
 
 def layer_kernel(
-    q_ref, k_ref, v_ref, f_ref, w_ref, s1_ref, fwd_ref, inv_ref, last_ref, tw_ref,
+    q_in, k_in, v_in, f_in, w_in, s1_in, fwd_in, inv_in, last_in, tw_in,
     out_ref,
+    q_ref, k_ref, v_ref, f_ref, s1_ref, fwd_ref, inv_ref, last_ref, tw_ref,
     prod, pbuf, qbuf, sig, filt, conv, fspec, gsend, gbuf, wbuf, acc, osend, obuf,
+    load_sem,
     p_send, p_recv, q_send, q_recv, w_send, w_recv, s_send, s_recv,
     g_send, g_recv, r_send, r_recv, l_send, l_recv, o_send, o_recv,
 ):
@@ -93,9 +95,29 @@
             device_id=device, device_id_type=MESH,
         )
         copy.start()
+        unsent.append(copy)
+        unreceived.append(copy)
         return copy
 
+    unsent, unreceived = [], []
+    scattered = False
+
+    def take_in(copies):
+        for copy in copies:
+            copy.wait_recv()
+            unreceived[:] = [other for other in unreceived if other is not copy]
+
     up, down = at(ctx, (z + 1) % RING, j), at(ctx, (z + RING - 1) % RING, j)
+    pairs = [
+        (k_in, k_ref), (v_in, v_ref), (f_in, f_ref), (s1_in, s1_ref), (fwd_in, fwd_ref),
+        (tw_in, tw_ref), (q_in, q_ref), (inv_in, inv_ref), (last_in, last_ref),
+        (w_in, wbuf.at[j]),
+    ]
+    loads = [
+        pltpu.make_async_copy(src, dst, load_sem.at[i]) for i, (src, dst) in enumerate(pairs)
+    ]
+    for copy in loads:
+        copy.start()
     barrier = pltpu.get_barrier_semaphore()
 
     def greet(i, _):
@@ -109,36 +131,35 @@
     pl.semaphore_signal(barrier, inc=1, device_id=up, device_id_type=MESH)
     pl.semaphore_signal(barrier, inc=1, device_id=down, device_id_type=MESH)
 
+    loads[0].wait()
+    loads[1].wait()
     prod[...] = (k_ref[...].astype(f32) * v_ref[...].astype(f32)).astype(bf16)
     pl.semaphore_wait(barrier, PLANE + 1)
 
-    waits = []
-    for refs in ((prod, pbuf, p_send, p_recv), (q_ref, qbuf, q_send, q_recv)):
-        src, dst, send_sem, recv_sem = refs
-        for i in range(1, CTX):
-            peer = (ctx + i) % CTX
-            waits.append(
-                send(src.at[peer], dst.at[ctx], send_sem.at[i], recv_sem.at[i], at(peer, z, j))
-            )
-    p_waits, q_waits = waits[: CTX - 1], waits[CTX - 1 :]
+    def spread(src, dst, send_sem, recv_sem):
+        peers = [(ctx + i) % CTX for i in range(1, CTX)]
+        return [
+            send(src.at[peer], dst.at[ctx], send_sem.at[i], recv_sem.at[i], at(peer, z, j))
+            for i, peer in enumerate(peers)
+        ]
+
+    p_waits = spread(prod, pbuf, p_send, p_recv)
     pbuf[ctx] = prod[ctx]
-    qbuf[ctx] = q_ref[ctx]
-
-    def turn(i, _):
-        rows = pl.ds(pl.multiple_of(i * 128, 128), 128)
-        wbuf[j, :, rows] = w_ref[rows, :].astype(f32).T.astype(bf16)
-        return 0
-
-    lax.fori_loop(0, D // 128, turn, 0)
+
     xr, xl = (x + 1) % 4, (x + 3) % 4
     right, left = at(ctx, z, xr * 2 + core), at(ctx, z, xl * 2 + core)
     sibling = at(ctx, z, x * 2 + 1 - core)
     j_right, j_left, j_far = xr * 2 + core, xl * 2 + core, ((x + 2) % 4) * 2 + core
     w_waits = [
-        send(wbuf.at[j], wbuf.at[j], w_send.at[0], w_recv.at[0], right),
-        send(wbuf.at[j], wbuf.at[j], w_send.at[1], w_recv.at[1], left),
+        send(w_in, wbuf.at[j], w_send.at[0], w_recv.at[0], right),
+        send(w_in, wbuf.at[j], w_send.at[1], w_recv.at[1], left),
     ]
-    s_waits = [send(wbuf.at[j], wbuf.at[j], s_send.at[0], s_recv.at[0], sibling)]
+    s_waits = [send(w_in, wbuf.at[j], s_send.at[0], s_recv.at[0], sibling)]
+    q_waits = spread(q_in, qbuf, q_send, q_recv)
+
+    for copy in loads[2:]:
+        copy.wait()
+    qbuf[ctx] = q_ref[ctx]
 
     own = pl.ds(pl.multiple_of(ctx * CHAN, CHAN), CHAN)
     for n in range(N1):
@@ -152,8 +173,7 @@
 
     lax.fori_loop(0, CHAN // BATCH, filter_step, 0)
 
-    for copy in p_waits:
-        copy.wait_recv()
+    take_in(p_waits)
     for n in range(N1):
         col = (n % 16) * N2
         sig[n * CHAN : (n + 1) * CHAN, :] = pbuf[n // 16, :, col : col + N2].astype(f32)
@@ -176,8 +196,7 @@
 
     lax.fori_loop(0, CHAN // BATCH, conv_step, 0)
 
-    for copy in q_waits:
-        copy.wait_recv()
+    take_in(q_waits)
     for n in range(N1):
         col = (n % 16) * N2
         gate = qbuf[n // 16, :, col : col + N2].astype(f32)
@@ -200,6 +219,7 @@
         return 0
 
     lax.fori_loop(1, PLANE, scatter, 0)
+    scattered = True
     gbuf[z, slot] = gsend[me]
 
     def arrived(i, _):
@@ -231,12 +251,12 @@
         lax.fori_loop(h * half, (h + 1) * half, arrived, 0)
         hops[0, h] = pass_on(0, h)
 
-    w_waits[0].wait_recv()
+    take_in([w_waits[0]])
     part = wbuf.at[j_left, pl.ds(0, 32)]
     w_waits.append(send(part, part, w_send.at[2], w_recv.at[2], right))
     part = wbuf.at[j_left]
     s_waits.append(send(part, part, s_send.at[1], s_recv.at[1], sibling))
-    w_waits[1].wait_recv()
+    take_in([w_waits[1]])
     part = wbuf.at[j_right, pl.ds(32, 32)]
     w_waits.append(send(part, part, w_send.at[3], w_recv.at[3], left))
     part = wbuf.at[j_right]
@@ -245,10 +265,7 @@
     def take(step):
         for h in range(2):
             ups, downs = hops[step, h]
-            if ups is not None:
-                ups.wait_recv()
-            if downs is not None:
-                downs.wait_recv()
+            take_in([copy for copy in (ups, downs) if copy is not None])
             if step < 3:
                 hops[step + 1, h] = pass_on(step + 1, h)
 
@@ -260,13 +277,11 @@
         acc[...] = term if first else acc[...] + term
 
     take(0)
-    w_waits[2].wait_recv()
-    w_waits[3].wait_recv()
+    take_in(w_waits[2:])
     part = wbuf.at[j_far]
     s_waits.append(send(part, part, s_send.at[3], s_recv.at[3], sibling))
     take(1)
-    for copy in s_waits:
-        copy.wait_recv()
+    take_in(s_waits)
     project(0, first=True)
     project(1)
     project(RING - 1)
@@ -286,18 +301,12 @@
             send(osend.at[peer], obuf.at[j], o_send.at[i], o_recv.at[i], at(ctx, z, peer))
         )
     obuf[j] = osend[j]
-    for copy in o_waits:
-        copy.wait_recv()
+    take_in(o_waits)
     for i in range(GROUP):
         out_ref[:, i * TOK : (i + 1) * TOK] = obuf[i]
 
-    for copy in p_waits + q_waits + w_waits + s_waits + o_waits:
+    for copy in unsent:
         copy.wait_send()
-    for ups, downs in hops.values():
-        if ups is not None:
-            ups.wait_send()
-        if downs is not None:
-            downs.wait_send()
 
     def sent(i, _):
         tile_copy(i).wait_send()
@@ -310,12 +319,18 @@
     tokens = SEQ // CTX
     split = (CTX, CHAN, tokens)
     dma = pltpu.SemaphoreType.DMA
+    consts = [jnp.asarray(t) for t in tables()]
     return pl.pallas_call(
         layer_kernel,
         out_shape=jax.ShapeDtypeStruct((CTX * CHAN, tokens), bf16),
-        in_specs=[pl.BlockSpec(memory_space=pltpu.VMEM)] * 10,
+        in_specs=[pl.BlockSpec(memory_space=pl.ANY)] * 10,
         out_specs=pl.BlockSpec(memory_space=pltpu.VMEM),
         scratch_shapes=[
+            pltpu.VMEM(split, bf16),
+            pltpu.VMEM(split, bf16),
+            pltpu.VMEM(split, bf16),
+            pltpu.VMEM((CTX * CHAN, SEQ), bf16),
+            *[pltpu.VMEM(t.shape, t.dtype) for t in consts],
             pltpu.VMEM(split, bf16),
             pltpu.VMEM(split, bf16),
             pltpu.VMEM(split, bf16),
@@ -329,22 +344,23 @@
             pltpu.VMEM((SLAB, TOK), f32),
             pltpu.VMEM((GROUP, 64, TOK), bf16),
             pltpu.VMEM((GROUP, 64, TOK), bf16),
-            dma((CTX,)), dma((CTX,)), dma((CTX,)), dma((CTX,)),
+            dma((10,)),
+            dma((CTX - 1,)), dma((CTX - 1,)), dma((CTX - 1,)), dma((CTX - 1,)),
             dma((4,)), dma((4,)), dma((4,)), dma((4,)),
             dma((PLANE,)), dma((PLANE,)),
             dma((4, 2)), dma((4, 2)), dma((4, 2)), dma((4, 2)),
             dma((GROUP,)), dma((GROUP,)),
         ],
         compiler_params=pltpu.CompilerParams(
-            collective_id=0, has_side_effects=True, vmem_limit_bytes=48 * 1024 * 1024
+            collective_id=0, has_side_effects=True, vmem_limit_bytes=56 * 1024 * 1024
         ),
     )(
         query_gate.reshape(split),
         key_gate.reshape(split),
         value_proj.reshape(split),
         filter_taps,
-        out_weight,
-        *[jnp.asarray(t) for t in tables()],
+        out_weight.T,
+        *consts,
     )
 
 

time: 67.9 us -> 60.4 us (0.89)
  local copies, waits for them, and re-layouts: 7.55 us -> 1.67 us
  Pallas kernels: 60 us -> 58.6 us
    unnamed x20 -> x1, local copies, waits for them, and re-layouts: 7.55 us -> 1.67 us
    pallas_call x1, Pallas kernels: 60 us -> 58.6 us  [per_device(): pl.pallas_call(layer_kernel, out_shape=jax.ShapeDtypeStruct((CTX * CHAN,...]
where the time goes in v2:
time: 60.4 us; the launch traced here: 60.2 us
  Pallas kernels  58.6 us (97%)
  local copies, waits for them, and re-layouts  1.67 us (3%)
    pallas_call x1, Pallas kernels, per_device(): pl.pallas_call(layer_kernel, out_shape=jax.ShapeDtypeStruct((CTX * CHAN,...  58.6 us
    unnamed x1, local copies, waits for them, and re-layouts  1.67 us

profile of v2, /device:TPU:1, one launch (start us, length us, event | category | flops | bytes accessed | tf_op | source)
XLA Modules:
  0.0 60.2 jit_solution(1850811672220054063)
XLA Ops:
  0.0 58.6 %shard_map.100 = bf16[64,2048]{1,0:T(8,128)(2,1)} custom-call(bf16[4,16,2048]{2,1,0:T(8,128)(2,1)} %bitcast.5, bf16[4,16,2048]{2,1,0:T(8,128)(2,1)} %bitcast.6, bf16[4,16,2048]{2,1,0:T(8,128)(2,1)} %bitcast.7, bf16[64,8192]{1,0:T(8,128)(2,1)} %f_in.1, bf16[64,4096]{1,0:T(8,128)(2,1)} %bitcast.4, bf16[128,128]{1,0:T(8,128)(2,1)} %constant.10.clone.s1_in, ...), custom_call_target="tpu_custom_call" | custom-call | tf_op jit(solution)/shard_map/pallas_call | solution.py:323
  58.6 1.7 %copy.12 = bf16[64,2048]{1,0:T(8,128)(2,1)} copy(bf16[64,2048]{1,0:T(8,128)(2,1)} %shard_map.100) | data formatting | bytes 524288

commit v3 on v2

--- a/solution.py
+++ b/solution.py
@@ -19,6 +19,8 @@
 TOK = 256
 D = 4096
 SLAB = D // RING
+PART = PLANE // 4
+NEAR = (0, 1, 3, 2)
 MESH = pl.DeviceIdType.MESH
 
 bf16 = jnp.bfloat16
@@ -43,8 +45,12 @@
     inv = two_parts(np.block([[second.real, -second.imag], [second.imag, second.real]]))
     high, low = two_parts(np.concatenate([first.real.T, first.imag.T], axis=1) / SEQ)
     last = np.concatenate([high, low], axis=1)
-    twist2 = np.concatenate([twist.real, twist.imag], axis=1).astype(np.float32)
-    return stage1, np.stack(fwd), np.stack(inv), last, twist2
+    twist2 = two_parts(np.concatenate([twist.real, twist.imag], axis=1))
+    stage1 = np.concatenate([stage1, np.zeros_like(stage1)], axis=1)
+    return np.concatenate([*fwd, *inv, last, stage1, *twist2], axis=0)
+
+
+FWD, INV, LAST, STAGE1, TWIST, END = np.cumsum([0, 4 * N2, 4 * N2, N1, 2 * N1, 2 * N1]).tolist()
 
 
 def dot(a, b):
@@ -58,7 +64,8 @@
 
 def dot3(x, table_ref):
     high, low = parts_of(x)
-    return dot(high, table_ref[0]) + (dot(low, table_ref[0]) + dot(high, table_ref[1]))
+    first, second = table_ref[: 2 * N2], table_ref[2 * N2 :]
+    return dot(high, first) + (dot(low, first) + dot(high, second))
 
 
 def spectrum(ref, c0, stage1, tw_re, tw_im, fwd_ref):
@@ -72,9 +79,9 @@
 
 
 def layer_kernel(
-    q_in, k_in, v_in, f_in, w_in, s1_in, fwd_in, inv_in, last_in, tw_in,
+    q_in, k_in, v_in, f_in, w_in, table_in,
     out_ref,
-    q_ref, k_ref, v_ref, f_ref, s1_ref, fwd_ref, inv_ref, last_ref, tw_ref,
+    q_ref, k_ref, v_ref, f_ref, table, tw_ref,
     prod, pbuf, qbuf, sig, filt, conv, fspec, gsend, gbuf, wbuf, acc, osend, obuf,
     load_sem,
     p_send, p_recv, q_send, q_recv, w_send, w_recv, s_send, s_recv,
@@ -109,8 +116,7 @@
 
     up, down = at(ctx, (z + 1) % RING, j), at(ctx, (z + RING - 1) % RING, j)
     pairs = [
-        (k_in, k_ref), (v_in, v_ref), (f_in, f_ref), (s1_in, s1_ref), (fwd_in, fwd_ref),
-        (tw_in, tw_ref), (q_in, q_ref), (inv_in, inv_ref), (last_in, last_ref),
+        (k_in, k_ref), (v_in, v_ref), (f_in, f_ref), (table_in, table), (q_in, q_ref),
         (w_in, wbuf.at[j]),
     ]
     loads = [
@@ -164,7 +170,10 @@
     own = pl.ds(pl.multiple_of(ctx * CHAN, CHAN), CHAN)
     for n in range(N1):
         filt[n * CHAN : (n + 1) * CHAN, :] = f_ref[own, n * N2 : (n + 1) * N2].astype(f32)
-    stage1 = s1_ref[...]
+    fwd_ref, inv_ref = table.at[FWD:INV], table.at[INV:LAST]
+    stage1 = table[STAGE1:TWIST, : 2 * N1]
+    twist = table[TWIST:END, :].astype(f32)
+    tw_ref[...] = twist[:N1] + twist[N1:]
     tw_re, tw_im = tw_ref[:, :N2], tw_ref[:, N2:]
 
     def filter_step(i, _):
@@ -184,7 +193,7 @@
         ss = spectrum(sig, c0, stage1, tw_re, tw_im, fwd_ref)
         fr, fi, sr, si = fs[:, :N2], fs[:, N2:], ss[:, :N2], ss[:, N2:]
         back = dot3(jnp.concatenate([fr * sr - fi * si, fr * si + fi * sr], axis=1), inv_ref)
-        last = last_ref[...]
+        last = table[LAST:STAGE1, :]
         for c in range(BATCH):
             re = back[c * N1 : (c + 1) * N1, :N2]
             im = back[c * N1 : (c + 1) * N1, N2:]
@@ -197,30 +206,33 @@
     lax.fori_loop(0, CHAN // BATCH, conv_step, 0)
 
     take_in(q_waits)
-    for n in range(N1):
-        col = (n % 16) * N2
-        gate = qbuf[n // 16, :, col : col + N2].astype(f32)
-        gsend[n // 2, :, (n % 2) * N2 : (n % 2 + 1) * N2] = (
-            gate * conv[n * CHAN : (n + 1) * CHAN, :]
-        ).astype(bf16)
-
     slot = j * CTX + ctx
 
-    def tile_copy(i):
-        peer = (me + i) % PLANE
+    def tile_copy(peer_ctx, peer_j):
+        peer = peer_ctx * GROUP + peer_j
         return pltpu.make_async_remote_copy(
-            src_ref=gsend.at[peer], dst_ref=gbuf.at[z, slot], send_sem=g_send.at[i],
-            recv_sem=g_recv.at[slot], device_id=at(peer // GROUP, z, peer % GROUP),
-            device_id_type=MESH,
+            src_ref=gsend.at[peer], dst_ref=gbuf.at[z, slot], send_sem=g_send.at[peer],
+            recv_sem=g_recv.at[slot], device_id=at(peer_ctx, z, peer_j), device_id_type=MESH,
         )
 
-    def scatter(i, _):
-        tile_copy(i).start()
-        return 0
-
-    lax.fori_loop(1, PLANE, scatter, 0)
+    def gated_tile(peer_ctx, peer_j):
+        halves = []
+        for n in range(2):
+            rows = pl.ds(pl.multiple_of((peer_ctx * 16 + peer_j * 2 + n) * CHAN, CHAN), CHAN)
+            cols = pl.ds(pl.multiple_of(peer_j * TOK + n * N2, N2), N2)
+            halves.append((qbuf[peer_ctx, :, cols].astype(f32) * conv[rows, :]).astype(bf16))
+        return jnp.concatenate(halves, axis=1)
+
+    def scatter(i, dx):
+        peer_ctx, peer_j = (ctx + i // 2) % CTX, (x + dx) % 4 * 2 + (core + i) % 2
+        gsend[peer_ctx * GROUP + peer_j] = gated_tile(peer_ctx, peer_j)
+        tile_copy(peer_ctx, peer_j).start()
+        return dx
+
+    for dx in NEAR:
+        lax.fori_loop(0 if dx else 1, PART, scatter, dx)
+    gbuf[z, slot] = gated_tile(ctx, j)
     scattered = True
-    gbuf[z, slot] = gsend[me]
 
     def arrived(i, _):
         @pl.when(i != slot)
@@ -232,23 +244,22 @@
 
         return 0
 
-    half = PLANE // 2
-
     def pass_on(step, h):
-        rows = pl.ds(h * half, half)
+        rows = pl.ds((x + 4 - NEAR[h]) % 4 * PART, PART)
         up_slab, down_slab = (z + RING - step) % RING, (z + step) % RING
         ups = downs = None
-        if step < 3 or h == 0:
+        if step < 3 or h < 2:
             part = gbuf.at[up_slab, rows]
             ups = send(part, part, r_send.at[step, h], r_recv.at[step, h], up)
-        if step < 3 or h == 1:
+        if step < 3 or h >= 2:
             part = gbuf.at[down_slab, rows]
             downs = send(part, part, l_send.at[step, h], l_recv.at[step, h], down)
         return ups, downs
 
     hops = {}
-    for h in range(2):
-        lax.fori_loop(h * half, (h + 1) * half, arrived, 0)
+    for h in range(4):
+        first = (x + 4 - NEAR[h]) % 4 * PART
+        lax.fori_loop(first, first + PART, arrived, 0)
         hops[0, h] = pass_on(0, h)
 
     take_in([w_waits[0]])
@@ -263,7 +274,7 @@
     s_waits.append(send(part, part, s_send.at[2], s_recv.at[2], sibling))
 
     def take(step):
-        for h in range(2):
+        for h in range(4):
             ups, downs = hops[step, h]
             take_in([copy for copy in (ups, downs) if copy is not None])
             if step < 3:
@@ -293,14 +304,15 @@
     take(3)
     project(4)
 
-    osend[...] = acc[...].reshape(GROUP, 64, TOK).astype(bf16)
     o_waits = []
     for i in range(1, GROUP):
         peer = (j + i) % GROUP
+        rows = pl.ds(pl.multiple_of(peer * 64, 64), 64)
+        osend[peer] = acc[rows, :].astype(bf16)
         o_waits.append(
             send(osend.at[peer], obuf.at[j], o_send.at[i], o_recv.at[i], at(ctx, z, peer))
         )
-    obuf[j] = osend[j]
+    obuf[j] = acc[pl.ds(pl.multiple_of(j * 64, 64), 64), :].astype(bf16)
     take_in(o_waits)
     for i in range(GROUP):
         out_ref[:, i * TOK : (i + 1) * TOK] = obuf[i]
@@ -309,7 +321,7 @@
         copy.wait_send()
 
     def sent(i, _):
-        tile_copy(i).wait_send()
+        tile_copy((ctx + i // GROUP) % CTX, (j + i) % GROUP).wait_send()
         return 0
 
     lax.fori_loop(1, PLANE, sent, 0)
@@ -319,18 +331,18 @@
     tokens = SEQ // CTX
     split = (CTX, CHAN, tokens)
     dma = pltpu.SemaphoreType.DMA
-    consts = [jnp.asarray(t) for t in tables()]
     return pl.pallas_call(
         layer_kernel,
         out_shape=jax.ShapeDtypeStruct((CTX * CHAN, tokens), bf16),
-        in_specs=[pl.BlockSpec(memory_space=pl.ANY)] * 10,
+        in_specs=[pl.BlockSpec(memory_space=pl.ANY)] * 6,
         out_specs=pl.BlockSpec(memory_space=pltpu.VMEM),
         scratch_shapes=[
             pltpu.VMEM(split, bf16),
             pltpu.VMEM(split, bf16),
             pltpu.VMEM(split, bf16),
             pltpu.VMEM((CTX * CHAN, SEQ), bf16),
-            *[pltpu.VMEM(t.shape, t.dtype) for t in consts],
+            pltpu.VMEM((END, 2 * N2), bf16),
+            pltpu.VMEM((N1, 2 * N2), f32),
             pltpu.VMEM(split, bf16),
             pltpu.VMEM(split, bf16),
             pltpu.VMEM(split, bf16),
@@ -344,15 +356,15 @@
             pltpu.VMEM((SLAB, TOK), f32),
             pltpu.VMEM((GROUP, 64, TOK), bf16),
             pltpu.VMEM((GROUP, 64, TOK), bf16),
-            dma((10,)),
+            dma((6,)),
             dma((CTX - 1,)), dma((CTX - 1,)), dma((CTX - 1,)), dma((CTX - 1,)),
             dma((4,)), dma((4,)), dma((4,)), dma((4,)),
             dma((PLANE,)), dma((PLANE,)),
-            dma((4, 2)), dma((4, 2)), dma((4, 2)), dma((4, 2)),
+            dma((4, 4)), dma((4, 4)), dma((4, 4)), dma((4, 4)),
             dma((GROUP,)), dma((GROUP,)),
         ],
         compiler_params=pltpu.CompilerParams(
-            collective_id=0, has_side_effects=True, vmem_limit_bytes=56 * 1024 * 1024
+            collective_id=0, has_side_effects=True, vmem_limit_bytes=54720 * 1024
         ),
     )(
         query_gate.reshape(split),
@@ -360,7 +372,7 @@
         value_proj.reshape(split),
         filter_taps,
         out_weight.T,
-        *consts,
+        jnp.asarray(tables()),
     )
 
 

time: 60.4 us -> 56.6 us (0.937)
  Pallas kernels: 58.6 us -> 54.8 us
    pallas_call x1, Pallas kernels: 58.6 us -> 54.8 us  [per_device(): pl.pallas_call(layer_kernel, out_shape=jax.ShapeDtypeStruct((CTX * CHAN,...]
    unnamed x1 -> x3, local copies, waits for them, and re-layouts: 1.67 us -> 1.65 us
where the time goes in v3:
time: 56.6 us; the launch traced here: 56.4 us
  Pallas kernels  54.8 us (97%)
  local copies, waits for them, and re-layouts  1.65 us (3%)
    pallas_call x1, Pallas kernels, per_device(): pl.pallas_call(layer_kernel, out_shape=jax.ShapeDtypeStruct((CTX * CHAN,...  54.8 us
    unnamed x3, local copies, waits for them, and re-layouts  1.65 us

profile of v3, /device:TPU:1, one launch (start us, length us, event | category | flops | bytes accessed | tf_op | source)
XLA Modules:
  0.0 56.4 jit_solution(9382015031668447891)
XLA Ops:
  0.0 0.0 copy-start
  0.0 0.9 %copy-done = bf16[64,2048]{1,0:T(8,128)(2,1)S(1)} copy-done((bf16[64,2048]{1,0:T(8,128)(2,1)S(1)}, bf16[64,2048]{1,0:T(8,128)(2,1)}, u32[]{:S(2)}) %copy-start) | copy-done | bytes 262168
  1.0 54.8 %shard_map.64 = bf16[64,2048]{1,0:T(8,128)(2,1)S(1)} custom-call(bf16[4,16,2048]{2,1,0:T(8,128)(2,1)S(1)} %bitcast.4, bf16[4,16,2048]{2,1,0:T(8,128)(2,1)} %bitcast.6, bf16[4,16,2048]{2,1,0:T(8,128)(2,1)} %bitcast.7, bf16[64,8192]{1,0:T(8,128)(2,1)} %f_in.1, bf16[64,4096]{1,0:T(8,128)(2,1)} %bitcast.5, bf16[1344,256]{1,0:T(8,128)(2,1)} %constant.2.clone.table_in), custom_call_target="tpu_custom_call" | custom-call | tf_op jit(solution)/shard_map/pallas_call | solution.py:334
  55.7 0.7 %copy.8 = bf16[64,2048]{1,0:T(8,128)(2,1)} copy(bf16[64,2048]{1,0:T(8,128)(2,1)S(1)} %shard_map.64) | data formatting | bytes 524288
Async XLA Ops:
  0.0 0.9 %copy-start = (bf16[64,2048]{1,0:T(8,128)(2,1)S(1)}, bf16[64,2048]{1,0:T(8,128)(2,1)}, u32[]{:S(2)}) copy-start(bf16[64,2048]{1,0:T(8,128)(2,1)} %param.6) | copy-start | bytes 786436

commit v4 on v3

--- a/solution.py
+++ b/solution.py
@@ -13,14 +13,13 @@
 CTX = 4
 GROUP = 8
 CHAN = 16
-BATCH = 4
+BATCH = 8
 RING = 8
 PLANE = CTX * GROUP
 TOK = 256
 D = 4096
 SLAB = D // RING
 PART = PLANE // 4
-NEAR = (0, 1, 3, 2)
 MESH = pl.DeviceIdType.MESH
 
 bf16 = jnp.bfloat16
@@ -156,11 +155,22 @@
     right, left = at(ctx, z, xr * 2 + core), at(ctx, z, xl * 2 + core)
     sibling = at(ctx, z, x * 2 + 1 - core)
     j_right, j_left, j_far = xr * 2 + core, xl * 2 + core, ((x + 2) % 4) * 2 + core
+    low, high = pl.ds(0, 32), pl.ds(32, 32)
+
+    def pass_weights(src, dst, i, device):
+        return send(src, dst, w_send.at[i], w_recv.at[i], device)
+
+    s_waits = []
+
+    def to_sibling(src, dst):
+        i = len(s_waits)
+        s_waits.append(send(src, dst, s_send.at[i], s_recv.at[i], sibling))
+
     w_waits = [
-        send(w_in, wbuf.at[j], w_send.at[0], w_recv.at[0], right),
-        send(w_in, wbuf.at[j], w_send.at[1], w_recv.at[1], left),
+        pass_weights(w_in.at[low], wbuf.at[j, low], 0, right),
+        pass_weights(w_in.at[high], wbuf.at[j, high], 1, left),
     ]
-    s_waits = [send(w_in, wbuf.at[j], s_send.at[0], s_recv.at[0], sibling)]
+    to_sibling(w_in, wbuf.at[j])
     q_waits = spread(q_in, qbuf, q_send, q_recv)
 
     for copy in loads[2:]:
@@ -168,8 +178,15 @@
     qbuf[ctx] = q_ref[ctx]
 
     own = pl.ds(pl.multiple_of(ctx * CHAN, CHAN), CHAN)
-    for n in range(N1):
-        filt[n * CHAN : (n + 1) * CHAN, :] = f_ref[own, n * N2 : (n + 1) * N2].astype(f32)
+
+    def widen_filter(i, _):
+        for k in range(CTX):
+            n = k * 16 + i
+            rows = pl.ds(pl.multiple_of(n * CHAN, CHAN), CHAN)
+            filt[rows, :] = f_ref[own, pl.ds(pl.multiple_of(n * N2, N2), N2)].astype(f32)
+        return 0
+
+    lax.fori_loop(0, 16, widen_filter, 0)
     fwd_ref, inv_ref = table.at[FWD:INV], table.at[INV:LAST]
     stage1 = table[STAGE1:TWIST, : 2 * N1]
     twist = table[TWIST:END, :].astype(f32)
@@ -183,9 +200,14 @@
     lax.fori_loop(0, CHAN // BATCH, filter_step, 0)
 
     take_in(p_waits)
-    for n in range(N1):
-        col = (n % 16) * N2
-        sig[n * CHAN : (n + 1) * CHAN, :] = pbuf[n // 16, :, col : col + N2].astype(f32)
+
+    def widen_signal(i, _):
+        for k in range(CTX):
+            rows = pl.ds(pl.multiple_of((k * 16 + i) * CHAN, CHAN), CHAN)
+            sig[rows, :] = pbuf[k, :, pl.ds(pl.multiple_of(i * N2, N2), N2)].astype(f32)
+        return 0
+
+    lax.fori_loop(0, 16, widen_signal, 0)
 
     def conv_step(i, _):
         c0 = i * BATCH
@@ -224,13 +246,15 @@
         return jnp.concatenate(halves, axis=1)
 
     def scatter(i, dx):
-        peer_ctx, peer_j = (ctx + i // 2) % CTX, (x + dx) % 4 * 2 + (core + i) % 2
+        peer_ctx, peer_j = (ctx + i // 2) % CTX, (x + 4 + dx) % 4 * 2 + (core + i) % 2
         gsend[peer_ctx * GROUP + peer_j] = gated_tile(peer_ctx, peer_j)
         tile_copy(peer_ctx, peer_j).start()
         return dx
 
-    for dx in NEAR:
-        lax.fori_loop(0 if dx else 1, PART, scatter, dx)
+    mate = 1 - 2 * (x % 2)
+    lax.fori_loop(1, PART, scatter, 0)
+    for dx in (mate, 4 - mate, 2):
+        lax.fori_loop(0, PART, scatter, dx)
     gbuf[z, slot] = gated_tile(ctx, j)
     scattered = True
 
@@ -244,63 +268,62 @@
 
         return 0
 
+    near = x // 2 * 2 * PART
+    firsts = (x * PART, (x + mate) * PART, 2 * PART - near)
+
     def pass_on(step, h):
-        rows = pl.ds((x + 4 - NEAR[h]) % 4 * PART, PART)
+        rows = pl.ds(near if h == 3 else firsts[h], PART if h < 2 else 2 * PART)
         up_slab, down_slab = (z + RING - step) % RING, (z + step) % RING
-        ups = downs = None
-        if step < 3 or h < 2:
+        copies = []
+        if step < 3 or h == 3:
             part = gbuf.at[up_slab, rows]
-            ups = send(part, part, r_send.at[step, h], r_recv.at[step, h], up)
-        if step < 3 or h >= 2:
+            copies.append(send(part, part, r_send.at[step, h], r_recv.at[step, h], up))
+        if step < 3 or h == 2:
             part = gbuf.at[down_slab, rows]
-            downs = send(part, part, l_send.at[step, h], l_recv.at[step, h], down)
-        return ups, downs
-
-    hops = {}
-    for h in range(4):
-        first = (x + 4 - NEAR[h]) % 4 * PART
-        lax.fori_loop(first, first + PART, arrived, 0)
-        hops[0, h] = pass_on(0, h)
-
-    take_in([w_waits[0]])
-    part = wbuf.at[j_left, pl.ds(0, 32)]
-    w_waits.append(send(part, part, w_send.at[2], w_recv.at[2], right))
-    part = wbuf.at[j_left]
-    s_waits.append(send(part, part, s_send.at[1], s_recv.at[1], sibling))
-    take_in([w_waits[1]])
-    part = wbuf.at[j_right, pl.ds(32, 32)]
-    w_waits.append(send(part, part, w_send.at[3], w_recv.at[3], left))
-    part = wbuf.at[j_right]
-    s_waits.append(send(part, part, s_send.at[2], s_recv.at[2], sibling))
+            copies.append(send(part, part, l_send.at[step, h], l_recv.at[step, h], down))
+        return copies
+
+    hops = []
+    for h in range(3):
+        lax.fori_loop(firsts[h], firsts[h] + (PART if h < 2 else 2 * PART), arrived, 0)
+        hops.append(pass_on(0, h))
+    hops = [hops[0] + hops[1], hops[2]]
+
+    take_in(w_waits)
+    from_left, from_right = wbuf.at[j_left, low], wbuf.at[j_right, high]
+    w_waits = [
+        pass_weights(from_left, from_left, 2, right),
+        pass_weights(from_right, from_right, 3, left),
+        pass_weights(w_in.at[high], wbuf.at[j, high], 4, right),
+        pass_weights(w_in.at[low], wbuf.at[j, low], 5, left),
+    ]
+    to_sibling(from_left, from_left)
+    to_sibling(from_right, from_right)
 
     def take(step):
-        for h in range(4):
-            ups, downs = hops[step, h]
-            take_in([copy for copy in (ups, downs) if copy is not None])
+        for i, h in enumerate((3, 2)):
+            take_in(hops[i])
             if step < 3:
-                hops[step + 1, h] = pass_on(step + 1, h)
-
-    def project(offset, first=False):
-        slab = (z + offset) % RING
+                hops[i] = pass_on(step + 1, h)
+
+    def project(offset):
+        slab = (z + RING + offset) % RING
         cols = pl.ds(pl.multiple_of(slab * SLAB, SLAB), SLAB)
         weight = wbuf[:, :, cols].reshape(SLAB, SLAB)
         term = dot(weight, gbuf[slab].reshape(SLAB, TOK))
-        acc[...] = term if first else acc[...] + term
+        acc[...] += term
+        return 0
 
     take(0)
-    take_in(w_waits[2:])
-    part = wbuf.at[j_far]
-    s_waits.append(send(part, part, s_send.at[3], s_recv.at[3], sibling))
+    take_in(w_waits)
+    for part in (wbuf.at[j_left, high], wbuf.at[j_right, low], wbuf.at[j_far]):
+        to_sibling(part, part)
     take(1)
     take_in(s_waits)
-    project(0, first=True)
-    project(1)
-    project(RING - 1)
+    acc[...] = jnp.zeros_like(acc)
+    lax.fori_loop(0, 3, lambda i, _: project(i - i // 2 * 3), 0)
     take(2)
-    project(2)
-    project(RING - 2)
-    project(3)
-    project(RING - 3)
+    lax.fori_loop(0, 4, lambda i, _: project((2 + i // 2) * (1 - i % 2 * 2)), 0)
     take(3)
     project(4)
 
@@ -358,13 +381,13 @@
             pltpu.VMEM((GROUP, 64, TOK), bf16),
             dma((6,)),
             dma((CTX - 1,)), dma((CTX - 1,)), dma((CTX - 1,)), dma((CTX - 1,)),
-            dma((4,)), dma((4,)), dma((4,)), dma((4,)),
+            dma((6,)), dma((6,)), dma((6,)), dma((6,)),
             dma((PLANE,)), dma((PLANE,)),
             dma((4, 4)), dma((4, 4)), dma((4, 4)), dma((4, 4)),
             dma((GROUP,)), dma((GROUP,)),
         ],
         compiler_params=pltpu.CompilerParams(
-            collective_id=0, has_side_effects=True, vmem_limit_bytes=54720 * 1024
+            collective_id=0, has_side_effects=True, vmem_limit_bytes=54784 * 1024
         ),
     )(
         query_gate.reshape(split),

time: 56.6 us -> 57.9 us (1.023)
  Pallas kernels: 54.8 us -> 57.1 us
  local copies, waits for them, and re-layouts: 1.65 us -> 0.71 us
    pallas_call x1, Pallas kernels: 54.8 us -> 57.1 us  [per_device(): pl.pallas_call(layer_kernel, out_shape=jax.ShapeDtypeStruct((CTX * CHAN,...]
    unnamed x3 -> x1, local copies, waits for them, and re-layouts: 1.65 us -> 0.71 us
where the time goes in v4:
time: 57.9 us; the launch traced here: 57.8 us
  Pallas kernels  57.1 us (99%)
  local copies, waits for them, and re-layouts  0.71 us (1%)
    pallas_call x1, Pallas kernels, per_device(): pl.pallas_call(layer_kernel, out_shape=jax.ShapeDtypeStruct((CTX * CHAN,...  57.1 us

profile of v4, /device:TPU:1, one launch (start us, length us, event | category | flops | bytes accessed | tf_op | source)
XLA Modules:
  0.0 57.8 jit_solution(14156653365254975673)
XLA Ops:
  0.0 57.1 %shard_map.64 = bf16[64,2048]{1,0:T(8,128)(2,1)S(1)} custom-call(bf16[4,16,2048]{2,1,0:T(8,128)(2,1)} %bitcast.5, bf16[4,16,2048]{2,1,0:T(8,128)(2,1)} %bitcast.6, bf16[4,16,2048]{2,1,0:T(8,128)(2,1)} %bitcast.7, bf16[64,8192]{1,0:T(8,128)(2,1)} %f_in.1, bf16[64,4096]{1,0:T(8,128)(2,1)} %bitcast.4, bf16[1344,256]{1,0:T(8,128)(2,1)} %constant.2.clone.table_in), custom_call_target="tpu_custom_call" | custom-call | tf_op jit(solution)/shard_map/pallas_call | solution.py:357
  57.1 0.7 %copy.8 = bf16[64,2048]{1,0:T(8,128)(2,1)} copy(bf16[64,2048]{1,0:T(8,128)(2,1)S(1)} %shard_map.64) | data formatting | bytes 524288

commit v5 on v4

--- a/solution.py
+++ b/solution.py
@@ -20,6 +20,7 @@
 D = 4096
 SLAB = D // RING
 PART = PLANE // 4
+NEAR = (0, 1, 3, 2)
 MESH = pl.DeviceIdType.MESH
 
 bf16 = jnp.bfloat16
@@ -246,15 +247,13 @@
         return jnp.concatenate(halves, axis=1)
 
     def scatter(i, dx):
-        peer_ctx, peer_j = (ctx + i // 2) % CTX, (x + 4 + dx) % 4 * 2 + (core + i) % 2
+        peer_ctx, peer_j = (ctx + i // 2) % CTX, (x + dx) % 4 * 2 + (core + i) % 2
         gsend[peer_ctx * GROUP + peer_j] = gated_tile(peer_ctx, peer_j)
         tile_copy(peer_ctx, peer_j).start()
         return dx
 
-    mate = 1 - 2 * (x % 2)
-    lax.fori_loop(1, PART, scatter, 0)
-    for dx in (mate, 4 - mate, 2):
-        lax.fori_loop(0, PART, scatter, dx)
+    for dx in NEAR:
+        lax.fori_loop(0 if dx else 1, PART, scatter, dx)
     gbuf[z, slot] = gated_tile(ctx, j)
     scattered = True
 
@@ -268,26 +267,23 @@
 
         return 0
 
-    near = x // 2 * 2 * PART
-    firsts = (x * PART, (x + mate) * PART, 2 * PART - near)
-
     def pass_on(step, h):
-        rows = pl.ds(near if h == 3 else firsts[h], PART if h < 2 else 2 * PART)
+        rows = pl.ds((x + 4 - NEAR[h]) % 4 * PART, PART)
         up_slab, down_slab = (z + RING - step) % RING, (z + step) % RING
-        copies = []
-        if step < 3 or h == 3:
+        ups = downs = None
+        if step < 3 or h < 2:
             part = gbuf.at[up_slab, rows]
-            copies.append(send(part, part, r_send.at[step, h], r_recv.at[step, h], up))
-        if step < 3 or h == 2:
+            ups = send(part, part, r_send.at[step, h], r_recv.at[step, h], up)
+        if step < 3 or h >= 2:
             part = gbuf.at[down_slab, rows]
-            copies.append(send(part, part, l_send.at[step, h], l_recv.at[step, h], down))
-        return copies
-
-    hops = []
-    for h in range(3):
-        lax.fori_loop(firsts[h], firsts[h] + (PART if h < 2 else 2 * PART), arrived, 0)
-        hops.append(pass_on(0, h))
-    hops = [hops[0] + hops[1], hops[2]]
+            downs = send(part, part, l_send.at[step, h], l_recv.at[step, h], down)
+        return ups, downs
+
+    hops = {}
+    for h in range(4):
+        first = (x + 4 - NEAR[h]) % 4 * PART
+        lax.fori_loop(first, first + PART, arrived, 0)
+        hops[0, h] = pass_on(0, h)
 
     take_in(w_waits)
     from_left, from_right = wbuf.at[j_left, low], wbuf.at[j_right, high]
@@ -301,10 +297,11 @@
     to_sibling(from_right, from_right)
 
     def take(step):
-        for i, h in enumerate((3, 2)):
-            take_in(hops[i])
+        for h in range(4):
+            ups, downs = hops[step, h]
+            take_in([copy for copy in (ups, downs) if copy is not None])
             if step < 3:
-                hops[i] = pass_on(step + 1, h)
+                hops[step + 1, h] = pass_on(step + 1, h)
 
     def project(offset):
         slab = (z + RING + offset) % RING
@@ -314,15 +311,15 @@
         acc[...] += term
         return 0
 
+    acc[...] = jnp.zeros_like(acc)
     take(0)
+    take(1)
     take_in(w_waits)
     for part in (wbuf.at[j_left, high], wbuf.at[j_right, low], wbuf.at[j_far]):
         to_sibling(part, part)
-    take(1)
+    take(2)
     take_in(s_waits)
-    acc[...] = jnp.zeros_like(acc)
     lax.fori_loop(0, 3, lambda i, _: project(i - i // 2 * 3), 0)
-    take(2)
     lax.fori_loop(0, 4, lambda i, _: project((2 + i // 2) * (1 - i % 2 * 2)), 0)
     take(3)
     project(4)

time: 57.9 us -> 54.7 us (0.945)
  Pallas kernels: 57.1 us -> 53.9 us
    pallas_call x1, Pallas kernels: 57.1 us -> 53.9 us  [per_device(): pl.pallas_call(layer_kernel, out_shape=jax.ShapeDtypeStruct((CTX * CHAN,...]
where the time goes in v5:
time: 54.7 us; the launch traced here: 54.6 us
  Pallas kernels  53.9 us (99%)
  local copies, waits for them, and re-layouts  0.71 us (1%)
    pallas_call x1, Pallas kernels, per_device(): pl.pallas_call(layer_kernel, out_shape=jax.ShapeDtypeStruct((CTX * CHAN,...  53.9 us

profile of v5, /device:TPU:1, one launch (start us, length us, event | category | flops | bytes accessed | tf_op | source)
XLA Modules:
  0.0 54.6 jit_solution(17455373488819794690)
XLA Ops:
  0.0 53.9 %shard_map.64 = bf16[64,2048]{1,0:T(8,128)(2,1)S(1)} custom-call(bf16[4,16,2048]{2,1,0:T(8,128)(2,1)} %bitcast.5, bf16[4,16,2048]{2,1,0:T(8,128)(2,1)} %bitcast.6, bf16[4,16,2048]{2,1,0:T(8,128)(2,1)} %bitcast.7, bf16[64,8192]{1,0:T(8,128)(2,1)} %f_in.1, bf16[64,4096]{1,0:T(8,128)(2,1)} %bitcast.4, bf16[1344,256]{1,0:T(8,128)(2,1)} %constant.2.clone.table_in), custom_call_target="tpu_custom_call" | custom-call | tf_op jit(solution)/shard_map/pallas_call | solution.py:354
  53.9 0.7 %copy.8 = bf16[64,2048]{1,0:T(8,128)(2,1)} copy(bf16[64,2048]{1,0:T(8,128)(2,1)S(1)} %shard_map.64) | data formatting | bytes 524288

commit v6 on v5

--- a/solution.py
+++ b/solution.py
@@ -317,10 +317,21 @@
     take_in(w_waits)
     for part in (wbuf.at[j_left, high], wbuf.at[j_right, low], wbuf.at[j_far]):
         to_sibling(part, part)
+    sends_so_far = len(unsent)
     take(2)
     take_in(s_waits)
     lax.fori_loop(0, 3, lambda i, _: project(i - i // 2 * 3), 0)
     lax.fori_loop(0, 4, lambda i, _: project((2 + i // 2) * (1 - i % 2 * 2)), 0)
+    for copy in unsent[:sends_so_far]:
+        copy.wait_send()
+    del unsent[:sends_so_far]
+
+    def sent(i, _):
+        tile_copy((ctx + i // GROUP) % CTX, (j + i) % GROUP).wait_send()
+        return 0
+
+    lax.fori_loop(1, PLANE, sent, 0)
+
     take(3)
     project(4)
 
@@ -333,18 +344,14 @@
             send(osend.at[peer], obuf.at[j], o_send.at[i], o_recv.at[i], at(ctx, z, peer))
         )
     obuf[j] = acc[pl.ds(pl.multiple_of(j * 64, 64), 64), :].astype(bf16)
-    take_in(o_waits)
-    for i in range(GROUP):
-        out_ref[:, i * TOK : (i + 1) * TOK] = obuf[i]
+    out_ref[:, pl.ds(pl.multiple_of(j * TOK, TOK), TOK)] = obuf[j]
+    for i, copy in enumerate(o_waits):
+        take_in([copy])
+        source = (j + GROUP - 1 - i) % GROUP
+        out_ref[:, pl.ds(pl.multiple_of(source * TOK, TOK), TOK)] = obuf[source]
 
     for copy in unsent:
         copy.wait_send()
-
-    def sent(i, _):
-        tile_copy((ctx + i // GROUP) % CTX, (j + i) % GROUP).wait_send()
-        return 0
-
-    lax.fori_loop(1, PLANE, sent, 0)
 
 
 def per_device(query_gate, key_gate, value_proj, filter_taps, out_weight):

time: 54.7 us -> 54.3 us (level)
  no operation moved by 1% of the time
where the time goes in v6:
time: 54.3 us; the launch traced here: 54.2 us
  Pallas kernels  53.5 us (99%)
  local copies, waits for them, and re-layouts  0.71 us (1%)
    pallas_call x1, Pallas kernels, per_device(): pl.pallas_call(layer_kernel, out_shape=jax.ShapeDtypeStruct((CTX * CHAN,...  53.5 us

profile of v6, /device:TPU:1, one launch (start us, length us, event | category | flops | bytes accessed | tf_op | source)
XLA Modules:
  0.0 54.2 jit_solution(2178930436753914383)
XLA Ops:
  0.0 53.5 %shard_map.64 = bf16[64,2048]{1,0:T(8,128)(2,1)S(1)} custom-call(bf16[4,16,2048]{2,1,0:T(8,128)(2,1)} %bitcast.5, bf16[4,16,2048]{2,1,0:T(8,128)(2,1)} %bitcast.6, bf16[4,16,2048]{2,1,0:T(8,128)(2,1)} %bitcast.7, bf16[64,8192]{1,0:T(8,128)(2,1)} %f_in.1, bf16[64,4096]{1,0:T(8,128)(2,1)} %bitcast.4, bf16[1344,256]{1,0:T(8,128)(2,1)} %constant.2.clone.table_in), custom_call_target="tpu_custom_call" | custom-call | tf_op jit(solution)/shard_map/pallas_call | solution.py:361
  53.5 0.7 %copy.8 = bf16[64,2048]{1,0:T(8,128)(2,1)} copy(bf16[64,2048]{1,0:T(8,128)(2,1)S(1)} %shard_map.64) | data formatting | bytes 524288

commit v7 on v6

--- a/solution.py
+++ b/solution.py
@@ -13,7 +13,7 @@
 CTX = 4
 GROUP = 8
 CHAN = 16
-BATCH = 8
+BATCH = 16
 RING = 8
 PLANE = CTX * GROUP
 TOK = 256
@@ -172,7 +172,6 @@
         pass_weights(w_in.at[high], wbuf.at[j, high], 1, left),
     ]
     to_sibling(w_in, wbuf.at[j])
-    q_waits = spread(q_in, qbuf, q_send, q_recv)
 
     for copy in loads[2:]:
         copy.wait()
@@ -199,16 +198,20 @@
         return 0
 
     lax.fori_loop(0, CHAN // BATCH, filter_step, 0)
-
-    take_in(p_waits)
-
-    def widen_signal(i, _):
-        for k in range(CTX):
-            rows = pl.ds(pl.multiple_of((k * 16 + i) * CHAN, CHAN), CHAN)
-            sig[rows, :] = pbuf[k, :, pl.ds(pl.multiple_of(i * N2, N2), N2)].astype(f32)
-        return 0
-
-    lax.fori_loop(0, 16, widen_signal, 0)
+    q_waits = spread(q_in, qbuf, q_send, q_recv)
+
+
+    def widen_signal(i, part):
+        for k in range(4):
+            n = i * 4 + k
+            rows = pl.ds(pl.multiple_of((part * 16 + n) * CHAN, CHAN), CHAN)
+            sig[rows, :] = pbuf[part, :, pl.ds(pl.multiple_of(n * N2, N2), N2)].astype(f32)
+        return part
+
+    lax.fori_loop(0, 4, widen_signal, ctx)
+    for i in (0, 2, 1):
+        take_in([p_waits[i]])
+        lax.fori_loop(0, 4, widen_signal, (ctx + CTX - 1 - i) % CTX)
 
     def conv_step(i, _):
         c0 = i * BATCH

time: 54.3 us -> 53.7 us (0.989)
  Pallas kernels: 53.5 us -> 52.9 us
    pallas_call x1, Pallas kernels: 53.5 us -> 52.9 us  [per_device(): pl.pallas_call(layer_kernel, out_shape=jax.ShapeDtypeStruct((CTX * CHAN,...]
where the time goes in v7:
time: 53.7 us
  Pallas kernels  52.9 us (99%)
  local copies, waits for them, and re-layouts  0.71 us (1%)
    pallas_call x1, Pallas kernels, per_device(): pl.pallas_call(layer_kernel, out_shape=jax.ShapeDtypeStruct((CTX * CHAN,...  52.9 us

profile of v7, /device:TPU:1, one launch (start us, length us, event | category | flops | bytes accessed | tf_op | source)
XLA Modules:
  0.0 53.7 jit_solution(3932800053255564907)
XLA Ops:
  0.0 52.9 %shard_map.64 = bf16[64,2048]{1,0:T(8,128)(2,1)S(1)} custom-call(bf16[4,16,2048]{2,1,0:T(8,128)(2,1)} %bitcast.5, bf16[4,16,2048]{2,1,0:T(8,128)(2,1)} %bitcast.6, bf16[4,16,2048]{2,1,0:T(8,128)(2,1)} %bitcast.7, bf16[64,8192]{1,0:T(8,128)(2,1)} %f_in.1, bf16[64,4096]{1,0:T(8,128)(2,1)} %bitcast.4, bf16[1344,256]{1,0:T(8,128)(2,1)} %constant.2.clone.table_in), custom_call_target="tpu_custom_call" | custom-call | tf_op jit(solution)/shard_map/pallas_call | solution.py:364
  52.9 0.7 %copy.8 = bf16[64,2048]{1,0:T(8,128)(2,1)} copy(bf16[64,2048]{1,0:T(8,128)(2,1)S(1)} %shard_map.64) | data formatting | bytes 524288

commit v8 on v7

--- a/solution.py
+++ b/solution.py
@@ -65,7 +65,9 @@
 def dot3(x, table_ref):
     high, low = parts_of(x)
     first, second = table_ref[: 2 * N2], table_ref[2 * N2 :]
-    return dot(high, first) + (dot(low, first) + dot(high, second))
+    rows = x.shape[0]
+    both = dot(jnp.concatenate([high, low], axis=0), first)
+    return both[:rows] + (both[rows:] + dot(high, second))
 
 
 def spectrum(ref, c0, stage1, tw_re, tw_im, fwd_ref):
@@ -133,7 +135,7 @@
         )
         return 0
 
-    lax.fori_loop(0, PLANE - 1, greet, 0)
+    lax.fori_loop(0, PLANE - 1, greet, 0, unroll=True)
     pl.semaphore_signal(barrier, inc=1, device_id=up, device_id_type=MESH)
     pl.semaphore_signal(barrier, inc=1, device_id=down, device_id_type=MESH)
 

time: 53.7 us -> 53.7 us (level)
  no operation moved by 1% of the time
where the time goes in v8:
time: 53.7 us; the launch traced here: 53.6 us
  Pallas kernels  52.9 us (99%)
  local copies, waits for them, and re-layouts  0.71 us (1%)
    pallas_call x1, Pallas kernels, per_device(): pl.pallas_call(layer_kernel, out_shape=jax.ShapeDtypeStruct((CTX * CHAN,...  52.9 us

profile of v8, /device:TPU:1, one launch (start us, length us, event | category | flops | bytes accessed | tf_op | source)
XLA Modules:
  0.0 53.6 jit_solution(628016395770846259)
XLA Ops:
  0.0 52.9 %shard_map.64 = bf16[64,2048]{1,0:T(8,128)(2,1)S(1)} custom-call(bf16[4,16,2048]{2,1,0:T(8,128)(2,1)} %bitcast.5, bf16[4,16,2048]{2,1,0:T(8,128)(2,1)} %bitcast.6, bf16[4,16,2048]{2,1,0:T(8,128)(2,1)} %bitcast.7, bf16[64,8192]{1,0:T(8,128)(2,1)} %f_in.1, bf16[64,4096]{1,0:T(8,128)(2,1)} %bitcast.4, bf16[1344,256]{1,0:T(8,128)(2,1)} %constant.2.clone.table_in), custom_call_target="tpu_custom_call" | custom-call | tf_op jit(solution)/shard_map/pallas_call | solution.py:366
  52.9 0.7 %copy.8 = bf16[64,2048]{1,0:T(8,128)(2,1)} copy(bf16[64,2048]{1,0:T(8,128)(2,1)S(1)} %shard_map.64) | data formatting | bytes 524288

commit v9 on v8

--- a/solution.py
+++ b/solution.py
@@ -129,7 +129,7 @@
     barrier = pltpu.get_barrier_semaphore()
 
     def greet(i, _):
-        peer = (me + 1 + i) % PLANE
+        peer = (me + 1 + (i + 12) % (PLANE - 1)) % PLANE
         pl.semaphore_signal(
             barrier, inc=1, device_id=at(peer // GROUP, z, peer % GROUP), device_id_type=MESH
         )

time: 53.7 us -> 53.4 us (level)
  no operation moved by 1% of the time
where the time goes in v9:
time: 53.4 us; the launch traced here: 53.3 us
  Pallas kernels  52.6 us (99%)
  local copies, waits for them, and re-layouts  0.71 us (1%)
    pallas_call x1, Pallas kernels, per_device(): pl.pallas_call(layer_kernel, out_shape=jax.ShapeDtypeStruct((CTX * CHAN,...  52.6 us

profile of v9, /device:TPU:1, one launch (start us, length us, event | category | flops | bytes accessed | tf_op | source)
XLA Modules:
  0.0 53.3 jit_solution(5268813444708912748)
XLA Ops:
  0.0 52.6 %shard_map.64 = bf16[64,2048]{1,0:T(8,128)(2,1)S(1)} custom-call(bf16[4,16,2048]{2,1,0:T(8,128)(2,1)} %bitcast.5, bf16[4,16,2048]{2,1,0:T(8,128)(2,1)} %bitcast.6, bf16[4,16,2048]{2,1,0:T(8,128)(2,1)} %bitcast.7, bf16[64,8192]{1,0:T(8,128)(2,1)} %f_in.1, bf16[64,4096]{1,0:T(8,128)(2,1)} %bitcast.4, bf16[1344,256]{1,0:T(8,128)(2,1)} %constant.2.clone.table_in), custom_call_target="tpu_custom_call" | custom-call | tf_op jit(solution)/shard_map/pallas_call | solution.py:366
  52.6 0.7 %copy.8 = bf16[64,2048]{1,0:T(8,128)(2,1)} copy(bf16[64,2048]{1,0:T(8,128)(2,1)S(1)} %shard_map.64) | data formatting | bytes 524288
